TPU v7x, 256 devices: a whole 4x4x8 slice. The times are simulated.
256 devices in a mesh: zonal: 64 (over y_lo, x, z), merid: 4 (over y_hi, core).
Axes of the slice: x: 4, y: 4 (y_hi: 2, y_lo: 2; y = y_hi * 2 + y_lo), z: 8, core: 2. Of those that a mesh axis runs over, the one named last changes fastest.
Arguments:
- field: bfloat16 [64, 4096, 256], P('merid', 'zonal'), may hold values from -6 to 6
- weight_one: bfloat16 [3, 3, 256, 256], replicated, may hold values from -0.125 to 0.125
- bias_one: float32 [256], replicated, may hold values from -3 to 3
- weight_two: bfloat16 [3, 3, 256, 256], replicated, may hold values from -0.125 to 0.125
- bias_two: float32 [256], replicated, may hold values from -3 to 3
- depth_levels: int32 [64, 4096], P('merid', 'zonal'), may hold values from 0 to 64
- fold_partner: int32 [4096], replicated, may hold values from 0 to 4095, as said below
- cotangent: bfloat16 [64, 4096, 256], P('merid', 'zonal'), may hold values from -6 to 6
Outputs:
- output: bfloat16 [64, 4096, 256], P('merid', 'zonal')
- input_grad: bfloat16 [64, 4096, 256], P('merid', 'zonal')
- grad_one: float32 [3, 3, 256, 256], replicated
- grad_two: float32 [3, 3, 256, 256], replicated
Inputs may be any that keep to these rules, and one draw needn't show every extreme that they name: fold_partner[i] = (4095 - i + s) mod 4096 with one pivot offset s, 0 to 4095, for the whole table.
All inputs are finite; a program needn't handle non-finite values.
Results may differ from a plain program's by a relative error of at most 0.003.
Values may be sent and summed in bfloat16 or wider, within the bound.
No kernel may reach another device: no remote copies, remote signals or barrier semaphores. Data moves between devices by JAX's collectives and lax.ppermute only.
A program may use at most 128 MiB of HBM per device.

v0:
```python
import math
import jax
import jax.numpy as jnp
from jax import lax
from jax.sharding import PartitionSpec as P

LEV = 64


def with_halo(cells, sides, width, closed):
    for axis, dim in sides:
        count = lax.axis_size(axis)
        ends = count if closed else count - 1
        head = lax.slice_in_dim(cells, 0, width, axis=dim)
        tail = lax.slice_in_dim(cells, cells.shape[dim] - width, cells.shape[dim], axis=dim)
        cells = jnp.concatenate(
            [
                lax.ppermute(tail, axis, [(i, (i + 1) % count) for i in range(ends)]),
                cells,
                lax.ppermute(head, axis, [((i + 1) % count, i) for i in range(ends)]),
            ],
            axis=dim,
        )
    return cells


def level_mask(depth_levels, channels):
    level_index = lax.broadcasted_iota(jnp.int32, (1, 1, channels), 2) % LEV
    return (level_index < depth_levels[:, :, None]).astype(jnp.float32)


def fold_forward(top_row, fold_partner):
    columns = top_row.shape[0]
    whole_row = lax.all_gather(top_row, "zonal", axis=0, tiled=True)
    partners = lax.dynamic_slice_in_dim(fold_partner, lax.axis_index("zonal") * columns, columns, 0)
    return jnp.take(whole_row, partners, axis=0)


def fold_backward(fold_grad, fold_partner):
    columns = fold_grad.shape[0]
    whole_row = lax.all_gather(fold_grad.astype(jnp.bfloat16), "zonal", axis=0, tiled=True).astype(
        fold_grad.dtype
    )
    partners = lax.dynamic_slice_in_dim(fold_partner, lax.axis_index("zonal") * columns, columns, 0)
    return jnp.take(whole_row, partners, axis=0)


def pad_field(values, fold_partner, is_top):
    with_rows = with_halo(values, (("merid", 0),), 1, False)
    fold_row = fold_forward(values[-1], fold_partner)
    upper_row = jnp.where(is_top, fold_row, with_rows[-1])
    with_rows = jnp.concatenate([with_rows[:-1], upper_row[None]], axis=0)
    return with_halo(with_rows, (("zonal", 1),), 1, True)


def unpad_grad(grad_pad, fold_partner, is_top):
    sides = jnp.concatenate([grad_pad[:, :1], grad_pad[:, -1:]], axis=1)
    returned = with_halo(sides.astype(jnp.bfloat16), (("zonal", 1),), 1, True).astype(sides.dtype)
    inner = grad_pad[:, 1:-1]
    inner = inner.at[:, 0].add(returned[:, 0]).at[:, -1].add(returned[:, 3])
    rims = jnp.concatenate([inner[:1], inner[-1:]], axis=0)
    back_rows = with_halo(rims.astype(jnp.bfloat16), (("merid", 0),), 1, False).astype(rims.dtype)
    folded = fold_backward(inner[-1], fold_partner)
    top_added = back_rows[3] + jnp.where(is_top, folded, jnp.zeros_like(folded))
    middle = inner[1:-1]
    return middle.at[0].add(back_rows[0]).at[-1].add(top_added)


def patches_of(padded, rows, columns):
    pieces = [
        padded[row_step : row_step + rows, col_step : col_step + columns]
        for row_step in range(3)
        for col_step in range(3)
    ]
    return jnp.concatenate(pieces, axis=2).reshape(rows * columns, -1)


def transpose_conv(delta, flat_weight, rows, columns):
    channels = delta.shape[1]
    parts = lax.dot_general(
        delta, flat_weight, (((1,), (1,)), ((), ())), preferred_element_type=jnp.float32
    )
    parts = parts.reshape(rows, columns, 9, channels)
    grad_pad = jnp.zeros((rows + 2, columns + 2, channels), jnp.float32)
    for row_step in range(3):
        for col_step in range(3):
            grad_pad = grad_pad.at[row_step : row_step + rows, col_step : col_step + columns].add(
                parts[:, :, 3 * row_step + col_step]
            )
    return grad_pad


def kernel_grad(patches, delta):
    channels = delta.shape[1]
    summed = lax.dot_general(
        patches, delta, (((0,), (0,)), ((), ())), preferred_element_type=jnp.float32
    )
    return summed.reshape(3, 3, channels, channels)


def shards(
    field, weight_one, bias_one, weight_two, bias_two, depth_levels, fold_partner, cotangent
):
    rows, columns, channels = field.shape
    is_top = lax.axis_index("merid") == lax.axis_size("merid") - 1
    mask = level_mask(depth_levels, channels)
    flat_one = weight_one.reshape(9 * channels, channels)
    flat_two = weight_two.reshape(9 * channels, channels)
    patches_one = patches_of(pad_field(field, fold_partner, is_top), rows, columns)
    pre_one = (
        jnp.dot(patches_one, flat_one, preferred_element_type=jnp.float32).reshape(
            rows, columns, channels
        )
        + bias_one
    )
    hidden = (jax.nn.gelu(pre_one) * mask).astype(jnp.bfloat16)
    patches_two = patches_of(pad_field(hidden, fold_partner, is_top), rows, columns)
    pre_two = jnp.dot(patches_two, flat_two, preferred_element_type=jnp.float32).reshape(
        rows, columns, channels
    )
    output = ((field.astype(jnp.float32) + pre_two + bias_two) * mask).astype(jnp.bfloat16)
    masked_grad = cotangent.astype(jnp.float32) * mask
    delta_two = masked_grad.astype(jnp.bfloat16).reshape(rows * columns, channels)
    grad_two = kernel_grad(patches_two, delta_two)
    hidden_grad = unpad_grad(
        transpose_conv(delta_two, flat_two, rows, columns), fold_partner, is_top
    )
    _, gelu_back = jax.vjp(jax.nn.gelu, pre_one)
    delta_one = (
        gelu_back(hidden_grad * mask)[0].astype(jnp.bfloat16).reshape(rows * columns, channels)
    )
    grad_one = kernel_grad(patches_one, delta_one)
    field_grad = unpad_grad(
        transpose_conv(delta_one, flat_one, rows, columns), fold_partner, is_top
    )
    input_grad = (masked_grad + field_grad).astype(jnp.bfloat16)
    grad_one, grad_two = lax.psum((grad_one, grad_two), ("zonal", "merid"))
    scale = 1.0 / math.sqrt(rows * columns * lax.axis_size("zonal") * lax.axis_size("merid"))
    return (output, input_grad, grad_one * scale, grad_two * scale)


def solution(mesh):
    placed = (
        P("merid", "zonal", None),
        P(),
        P(),
        P(),
        P(),
        P("merid", "zonal"),
        P(),
        P("merid", "zonal", None),
    )
    return jax.shard_map(
        shards,
        mesh=mesh,
        in_specs=placed,
        out_specs=(P("merid", "zonal", None), P("merid", "zonal", None), P(), P()),
        check_vma=False,
    )
```

profile of v0, /device:TPU:97, one launch (start us, length us, event | category | flops | bytes accessed | tf_op | source)
XLA Modules:
  0.0 1509.0 jit_solution(12286972379343277605)
XLA Ops:
  7.2 1.5 fusion.52
  10.1 2.9 fusion.35
  14.0 2.7 copy-done.2
  16.6 2.4 fusion.27
  19.0 6.4 scatter-add.89
  26.8 4.3 add_select_fusion.1
  31.1 6.4 scatter-add.90
  37.5 1.4 fusion.26
  39.0 2.4 fusion.24
  41.3 5.1 scatter-add.94
  46.5 2.4 fusion.23
  48.8 5.1 scatter-add.95
  53.9 1.4 fusion.22
  55.4 2.4 fusion.20
  57.8 5.1 scatter-add.99
  62.9 2.4 fusion.19
  65.3 5.1 scatter-add.100
  70.5 2.9 collective-permute-start.8
  74.6 2.7 collective-permute-done.9
  77.4 1.6 scatter-add.101
  80.0 1.6 scatter-add.104
  81.7 1.5 fusion.48
  83.2 6.8 collective-permute-start
  90.1 1.9 collective-permute-start.1
  94.1 5.1 collective-permute-start.10
  99.3 1.9 collective-permute-start.11
  101.2 157.8 %all-gather.9.cloned.1.call-done = bf16[1,4096,256]{2,1,0:T(8,128)(2,1)} async-done(((bf16[1,64,256]{2,1,0:T(8,128)(2,1)}), bf16[1,4096,256]{2,1,0:T(8,128)(2,1)}) %all-gather.9.cloned.1.call-update) | async-done | bytes 2097168 | tf_op jit(solution)/shard_map/all_gather | solution.py:34
  259.0 2.5 gather_fusion
  262.9 3.3 collective-permute-start.3
  276.2 282.4 %all-gather.13.cloned.1.call-done = bf16[1,4096,256]{2,1,0:T(8,128)(2,1)} async-done(((bf16[1,64,256]{2,1,0:T(8,128)(2,1)}), bf16[1,4096,256]{2,1,0:T(8,128)(2,1)}) %all-gather.13.cloned.1.call-update) | async-done | bytes 2097168 | tf_op jit(solution)/shard_map/all_gather | solution.py:41
  558.5 3.9 bitcast_convert_fusion.1
  562.4 2.8 gather_fusion.2
  565.4 5.2 fusion.8
  571.3 2.5 fusion.33
  574.0 3.4 copy-done.3
  577.3 2.4 fusion.18
  579.7 6.4 scatter-add.110
  586.1 3.3 add_select_fusion
  589.4 3.3 scatter-add.111
  595.5 2.0 scatter-add.115
  598.9 2.0 scatter-add.116
  603.7 2.0 scatter-add.120
  607.1 2.0 scatter-add.121
  610.6 3.1 collective-permute-start.13
  619.2 50.8 %collective-permute-start.5 = (bf16[1,64,256]{2,1,0:T(8,128)(2,1)}, bf16[1,64,256]{2,1,0:T(8,128)(2,1)S(1)}, u32[]{:S(2)}, u32[]{:S(2)}) collective-permute-start(bf16[1,64,256]{2,1,0:T(8,128)(2,1)} %get-tuple-element.341), channel_id=1, source_target_pairs={{1,0},{2,1},{3,2},{5,4},{6,5},{7,6},{9,8},{10,9},{11,10},{13,12},{... | collective-permute-start | bytes 98312 | tf_op jit(solution)/shard_map/ppermute | solution.py:20
  670.0 4.3 collective-permute-start.4
  674.3 6.8 copy.30
  681.1 187.6 %all-gather.11.cloned.1.call-done = bf16[1,4096,256]{2,1,0:T(8,128)(2,1)} async-done(((bf16[1,64,256]{2,1,0:T(8,128)(2,1)}), bf16[1,4096,256]{2,1,0:T(8,128)(2,1)}) %all-gather.11.cloned.1.call-update) | async-done | bytes 2097168 | tf_op jit(solution)/shard_map/all_gather | solution.py:34
  868.7 2.6 gather_fusion.1
  871.5 2.0 collective-permute-start.6
  873.5 2.5 collective-permute-start.7
  876.0 5.1 fusion.55
  882.4 2.2 copy-done.5
  884.6 6.8 copy.31
  891.4 5.1 fusion.56
  897.3 52.6 %collective-permute-start.14 = (bf16[1,64,256]{2,1,0:T(8,128)(2,1)S(1)}, bf16[1,64,256]{2,1,0:T(8,128)(2,1)S(1)}, u32[]{:S(2)}, u32[]{:S(2)}) collective-permute-start(bf16[1,64,256]{2,1,0:T(8,128)(2,1)S(1)} %copy-done.14), channel_id=1, source_target_pairs={{0,1},{1,2},{2,3},{4,5},{5,6},{6,7},{8,9},{9,10},{10,11},{12,13},{... | collective-permute-start | bytes 98312 | tf_op jit(solution)/shard_map/ppermute | solution.py:18
  949.9 1.9 collective-permute-start.15
  951.9 4.7 collective-permute-done.15
  956.7 211.5 %all-gather.15.cloned.1.call-done = bf16[1,4096,256]{2,1,0:T(8,128)(2,1)} async-done(((bf16[1,64,256]{2,1,0:T(8,128)(2,1)}), bf16[1,4096,256]{2,1,0:T(8,128)(2,1)}) %all-gather.15.cloned.1.call-update) | async-done | bytes 2097168 | tf_op jit(solution)/shard_map/all_gather | solution.py:41
  1168.2 3.9 bitcast_convert_fusion
  1172.0 3.0 gather_fusion.3
  1176.3 4.5 fusion.1
  1180.8 316.5 %all-reduce.5.cloned.1.call-done = (f32[3,3,256,256]{3,2,1,0:T(8,128)}, f32[3,3,256,256]{3,2,1,0:T(8,128)}) async-done(((f32[3,3,256,256]{3,2,1,0:T(8,128)}, f32[3,3,256,256]{3,2,1,0:T(8,128)}), (f32[3,3,256,256]{3,2,1,0:T(8,128)}, f32[3,3,256,256]{3,2,1,0:T(8,128)})) %all-reduce.5.cloned.1.call-update) | async-done | bytes 4718608 | tf_op jit(solution)/shard_map/psum | solution.py:137
  1497.3 5.1 broadcast_multiply_fusion
  (148 shorter events, 39.2 us)
Async XLA Ops:
  7.2 558.2 %copy-start = (bf16[3,3,256,256]{3,2,1,0:T(8,128)(2,1)S(1)}, bf16[3,3,256,256]{3,2,1,0:T(8,128)(2,1)}, u32[]{:S(2)}) copy-start(bf16[3,3,256,256]{3,2,1,0:T(8,128)(2,1)} %param.65) | copy-start | bytes 3538948
  7.2 251.8 %all-gather.9.cloned.1.call-start = ((), (), s32[]{:S(2)}) async-start(), calls=%async_computation | async-start | bytes 2129920 | tf_op jit(solution)/shard_map/all_gather | solution.py:34
  8.7 549.8 %all-gather.13.cloned.1.call-start = ((), (), s32[]{:S(2)}) async-start(), calls=%async_computation.2 | async-start | bytes 2129920 | tf_op jit(solution)/shard_map/all_gather | solution.py:41
  8.8 556.6 %copy-start.25 = (s32[256]{0:T(256)}, s32[256]{0:T(256)S(1)}, u32[]{:S(2)}) copy-start(s32[256]{0:T(256)S(1)} %and_select_fusion) | copy-start | bytes 3076
  10.1 2.9 copy-start.8
  13.0 3.7 copy-start.2
  16.6 9.5 copy-start.27
  70.4 12.8 copy-start.17
  70.5 4.1 collective-permute-start.8
  73.4 188.2 %copy-start.4 = (bf16[16,64,256]{2,1,0:T(8,128)(2,1)S(1)}, bf16[16,64,256]{2,1,0:T(8,128)(2,1)}, u32[]{:S(2)}) copy-start(bf16[16,64,256]{2,1,0:T(8,128)(2,1)} %param.64) | copy-start | bytes 1572868
  73.4 3.8 collective-permute-start.9
  83.2 183.1 %copy-start.13 = (bf16[1,64,256]{2,1,0:T(8,128)(2,1)S(1)}, bf16[1,64,256]{2,1,0:T(8,128)(2,1)}, u32[]{:S(2)}) copy-start(bf16[1,64,256]{2,1,0:T(8,128)(2,1)} %get-tuple-element.324) | copy-start | bytes 98308
  83.2 785.5 %all-gather.11.cloned.1.call-start = ((), (), s32[]{:S(2)}) async-start(), calls=%async_computation.1 | async-start | bytes 2129920 | tf_op jit(solution)/shard_map/all_gather | solution.py:34
  83.2 178.4 %collective-permute-start = (bf16[1,64,256]{2,1,0:T(8,128)(2,1)S(1)}, bf16[1,64,256]{2,1,0:T(8,128)(2,1)S(1)}, u32[]{:S(2)}, u32[]{:S(2)}) collective-permute-start(bf16[1,64,256]{2,1,0:T(8,128)(2,1)S(1)} %copy-done.17), channel_id=1, source_target_pairs={{0,1},{1,2},{2,3},{4,5},{5,6},{6,7},{8,9},{9,10},{10,11},{12,13},{... | collective-permute-start | bytes 98312 | tf_op jit(solution)/shard_map/ppermute | solution.py:18
  90.1 171.5 %collective-permute-start.1 = (bf16[1,64,256]{2,1,0:T(8,128)(2,1)S(1)}, bf16[1,64,256]{2,1,0:T(8,128)(2,1)S(1)}, u32[]{:S(2)}, u32[]{:S(2)}) collective-permute-start(bf16[1,64,256]{2,1,0:T(8,128)(2,1)S(1)} %get-tuple-element.343), channel_id=1, source_target_pairs={{1,0},{2,1},{3,2},{5,4},{6,5},{7,6},{9,8},{10,9},{11,10},{13,12},{... | collective-permute-start | bytes 98312 | tf_op jit(solution)/shard_map/ppermute | solution.py:20
  92.8 472.5 %copy-start.22 = (pred[64]{0:T(512)(128)(4,1)}, pred[64]{0:T(512)(128)(4,1)S(1)}, u32[]{:S(2)}) copy-start(pred[64]{0:T(512)(128)(4,1)S(1)} %get-tuple-element.320) | copy-start | bytes 196
  92.8 469.7 %copy-start.24 = (s32[1024]{0:T(1024)}, s32[1024]{0:T(1024)S(1)}, u32[]{:S(2)}) copy-start(s32[1024]{0:T(1024)S(1)} %pad_clamp_fusion) | copy-start | bytes 12292
  94.1 172.1 %collective-permute-start.10 = (bf16[1,64,256]{2,1,0:T(8,128)(2,1)}, bf16[1,64,256]{2,1,0:T(8,128)(2,1)S(1)}, u32[]{:S(2)}, u32[]{:S(2)}) collective-permute-start(bf16[1,64,256]{2,1,0:T(8,128)(2,1)} %get-tuple-element.324), channel_id=1, source_target_pairs={{0,1},{1,2},{2,3},{4,5},{5,6},{6,7},{8,9},{9,10},{10,11},{12,13},{... | collective-permute-start | bytes 98312 | tf_op jit(solution)/shard_map/ppermute | solution.py:18
  99.3 167.0 %collective-permute-start.11 = (bf16[1,64,256]{2,1,0:T(8,128)(2,1)S(1)}, bf16[1,64,256]{2,1,0:T(8,128)(2,1)S(1)}, u32[]{:S(2)}, u32[]{:S(2)}) collective-permute-start(bf16[1,64,256]{2,1,0:T(8,128)(2,1)S(1)} %get-tuple-element.325), channel_id=1, source_target_pairs={{1,0},{2,1},{3,2},{5,4},{6,5},{7,6},{9,8},{10,9},{11,10},{13,12},{... | collective-permute-start | bytes 98312 | tf_op jit(solution)/shard_map/ppermute | solution.py:20
  261.7 5.7 collective-permute-start.2
  262.9 4.4 collective-permute-start.3
  276.2 289.3 %copy-start.20 = (s32[16,64]{1,0:T(8,128)S(1)}, s32[16,64]{1,0:T(8,128)}, u32[]{:S(2)}) copy-start(s32[16,64]{1,0:T(8,128)} %param.69) | copy-start | bytes 12292
  276.2 289.3 %copy-start.28 = (f32[256]{0:T(256)S(1)}, f32[256]{0:T(256)}, u32[]{:S(2)}) copy-start(f32[256]{0:T(256)} %param.66) | copy-start | bytes 3076
  571.2 596.9 %all-gather.15.cloned.1.call-start = ((), (), s32[]{:S(2)}) async-start(), calls=%async_computation.3 | async-start | bytes 2129920 | tf_op jit(solution)/shard_map/all_gather | solution.py:41
  573.8 3.6 copy-start.3
  609.3 5.5 copy-start.15
  609.3 5.5 copy-start.16
  609.3 5.5 collective-permute-start.12
  610.6 4.2 collective-permute-start.13
  614.7 0.6 copy-start.18
  615.3 0.6 copy-start.19
  618.4 62.7 %copy-start.6 = (f32[18,64,256]{2,1,0:T(8,128)}, f32[18,64,256]{2,1,0:T(8,128)S(1)}, u32[]{:S(2)}) copy-start(f32[18,64,256]{2,1,0:T(8,128)S(1)} %scatter-add.125) | copy-start | bytes 3538948
  619.1 878.2 %all-reduce.5.cloned.1.call-start = ((), (), s32[]{:S(2)}) async-start(), calls=%async_computation.4 | async-start | bytes 9437184 | tf_op jit(solution)/shard_map/psum | solution.py:137
  619.2 252.2 %collective-permute-start.5 = (bf16[1,64,256]{2,1,0:T(8,128)(2,1)}, bf16[1,64,256]{2,1,0:T(8,128)(2,1)S(1)}, u32[]{:S(2)}, u32[]{:S(2)}) collective-permute-start(bf16[1,64,256]{2,1,0:T(8,128)(2,1)} %get-tuple-element.341), channel_id=1, source_target_pairs={{1,0},{2,1},{3,2},{5,4},{6,5},{7,6},{9,8},{10,9},{11,10},{13,12},{... | collective-permute-start | bytes 98312 | tf_op jit(solution)/shard_map/ppermute | solution.py:20
  670.0 201.4 %collective-permute-start.4 = (bf16[1,64,256]{2,1,0:T(8,128)(2,1)}, bf16[1,64,256]{2,1,0:T(8,128)(2,1)S(1)}, u32[]{:S(2)}, u32[]{:S(2)}) collective-permute-start(bf16[1,64,256]{2,1,0:T(8,128)(2,1)} %get-tuple-element.340), channel_id=1, source_target_pairs={{0,1},{1,2},{2,3},{4,5},{5,6},{6,7},{8,9},{9,10},{10,11},{12,13},{... | collective-permute-start | bytes 98312 | tf_op jit(solution)/shard_map/ppermute | solution.py:18
  674.3 197.0 %copy-start.23 = (pred[64]{0:T(512)(128)(4,1)S(1)}, pred[64]{0:T(512)(128)(4,1)}, u32[]{:S(2)}) copy-start(pred[64]{0:T(512)(128)(4,1)} %copy-done.22) | copy-start | bytes 196
  674.3 201.7 %copy-start.12 = (bf16[16,64,256]{2,1,0:T(8,128)(2,1)S(1)}, bf16[16,64,256]{2,1,0:T(8,128)(2,1)}, u32[]{:S(2)}) copy-start(bf16[16,64,256]{2,1,0:T(8,128)(2,1)} %get-tuple-element.326) | copy-start | bytes 1572868
  871.5 9.7 collective-permute-start.6
  873.5 7.7 collective-permute-start.7
  882.4 2.2 copy-start.5
  884.6 6.8 copy-start.9
  896.5 0.8 copy-start.14
  896.5 55.3 %copy-start.7 = (f32[18,64,256]{2,1,0:T(8,128)S(1)}, f32[18,64,256]{2,1,0:T(8,128)}, u32[]{:S(2)}) copy-start(f32[18,64,256]{2,1,0:T(8,128)} %copy-done.6) | copy-start | bytes 3538948
  897.3 54.6 %collective-permute-start.14 = (bf16[1,64,256]{2,1,0:T(8,128)(2,1)S(1)}, bf16[1,64,256]{2,1,0:T(8,128)(2,1)S(1)}, u32[]{:S(2)}, u32[]{:S(2)}) collective-permute-start(bf16[1,64,256]{2,1,0:T(8,128)(2,1)S(1)} %copy-done.14), channel_id=1, source_target_pairs={{0,1},{1,2},{2,3},{4,5},{5,6},{6,7},{8,9},{9,10},{10,11},{12,13},{... | collective-permute-start | bytes 98312 | tf_op jit(solution)/shard_map/ppermute | solution.py:18
  949.9 6.7 collective-permute-start.15
  956.6 218.5 %copy-start.10 = (bf16[16,64,256]{2,1,0:T(8,128)(2,1)S(1)}, bf16[16,64,256]{2,1,0:T(8,128)(2,1)}, u32[]{:S(2)}) copy-start(bf16[16,64,256]{2,1,0:T(8,128)(2,1)} %param.71) | copy-start | bytes 1572868
  956.6 218.5 %copy-start.21 = (s32[16,64]{1,0:T(8,128)S(1)}, s32[16,64]{1,0:T(8,128)}, u32[]{:S(2)}) copy-start(s32[16,64]{1,0:T(8,128)} %param.69) | copy-start | bytes 12292
  956.6 218.5 %copy-start.26 = (s32[256]{0:T(256)S(1)}, s32[256]{0:T(256)}, u32[]{:S(2)}) copy-start(s32[256]{0:T(256)} %copy-done.25) | copy-start | bytes 3076
  1172.0 4.2 copy-start.29
  1175.0 1.3 copy-start.11
  1497.3 5.1 copy-start.1
Sparse Core Ops, SparseCore 0:
  10.4 248.6 all-gather.8
  261.4 297.1 all-gather.12
  571.4 297.2 all-gather.10
  870.3 297.7 all-gather.14
  1174.2 323.0 all-reduce.4
where the time goes:
time: 1510 us
  waiting for transfers between devices  1160 us (77%)
  starting transfers between devices  142 us (9%)
  local copies, waits for them, and re-layouts  106 us (7%)
  other arithmetic  56.4 us (4%)
  matrix products  25.3 us (2%)
    all_gather x2, waiting for transfers between devices, fold_backward(): lax.all_gather(fold_grad.astype(jnp.bfloat16), 'zonal', axis=0, tiled=True)  494 us
    all_gather x2, waiting for transfers between devices, fold_forward(): whole_row = lax.all_gather(top_row, 'zonal', axis=0, tiled=True)  345 us
    psum x1, waiting for transfers between devices, shards(): grad_one, grad_two = lax.psum((grad_one, grad_two), ('zonal', 'merid'))  317 us
    ppermute x8, starting transfers between devices, with_halo(): lax.ppermute(tail, axis, [(i, (i + 1) % count) for i in range(ends)])  76.3 us
    ppermute x8, starting transfers between devices, with_halo(): lax.ppermute(head, axis, [((i + 1) % count, i) for i in range(ends)])  65.5 us
    scatter-add x14, local copies, waits for them, and re-layouts, transpose_conv(): grad_pad.at[row_step:row_step + rows, col_step:col_step + columns]  51.2 us
  transfers between devices with their start and end apart: 21, of which 9 were waited for; matrix products, arithmetic and copies ran while one was open for 10% of the time, Pallas kernels for 0%

commit v1 on v0

--- a/solution.py
+++ b/solution.py
@@ -134,7 +134,7 @@
         transpose_conv(delta_one, flat_one, rows, columns), fold_partner, is_top
     )
     input_grad = (masked_grad + field_grad).astype(jnp.bfloat16)
-    grad_one, grad_two = lax.psum((grad_one, grad_two), ("zonal", "merid"))
+    grad_one, grad_two = lax.psum(lax.psum((grad_one, grad_two), "zonal"), "merid")
     scale = 1.0 / math.sqrt(rows * columns * lax.axis_size("zonal") * lax.axis_size("merid"))
     return (output, input_grad, grad_one * scale, grad_two * scale)
 

time: 1510 us -> 1990 us (1.32)
  waiting for transfers between devices: 1160 us -> 1620 us
  local copies, waits for them, and re-layouts: 106 us -> 128 us
    psum x1 -> x2, waiting for transfers between devices: 317 us -> 698 us  [the longest x1 553 us: shards(): lax.psum((grad_one, grad_two), 'zonal')]
    all_gather x2, waiting for transfers between devices: 345 us -> 393 us  [fold_forward(): whole_row = lax.all_gather(top_row, 'zonal', axis=0, tiled=True)]
    all_gather x2, waiting for transfers between devices: 494 us -> 521 us  [fold_backward(): lax.all_gather(fold_grad.astype(jnp.bfloat16), 'zonal', axis=0, tiled=True)]
  transfers between devices with their start and end apart: 21 -> 22, of which waited for: 9 -> 10; matrix products, arithmetic and copies ran while one was open for 10% -> 9% of each run, Pallas kernels for 0% -> 0%
where the time goes in v1:
time: 1990 us
  waiting for transfers between devices  1620 us (81%)
  starting transfers between devices  138 us (7%)
  local copies, waits for them, and re-layouts  128 us (6%)
  other arithmetic  65.2 us (3%)
  matrix products  23.6 us (1%)
    psum x1, waiting for transfers between devices, shards(): lax.psum((grad_one, grad_two), 'zonal')  553 us
    all_gather x2, waiting for transfers between devices, fold_backward(): lax.all_gather(fold_grad.astype(jnp.bfloat16), 'zonal', axis=0, tiled=True)  521 us
    all_gather x2, waiting for transfers between devices, fold_forward(): whole_row = lax.all_gather(top_row, 'zonal', axis=0, tiled=True)  393 us
    psum x1, waiting for transfers between devices, shards(): lax.psum(lax.psum((grad_one, grad_two), 'zonal'), 'merid')  145 us
    ppermute x8, starting transfers between devices, with_halo(): lax.ppermute(tail, axis, [(i, (i + 1) % count) for i in range(ends)])  74.2 us
    scatter-add x14, local copies, waits for them, and re-layouts, transpose_conv(): grad_pad.at[row_step:row_step + rows, col_step:col_step + columns]  67 us
    ppermute x8, starting transfers between devices, with_halo(): lax.ppermute(head, axis, [((i + 1) % count, i) for i in range(ends)])  63.3 us
  transfers between devices with their start and end apart: 22, of which 10 were waited for; matrix products, arithmetic and copies ran while one was open for 9% of the time, Pallas kernels for 0%

profile of v1, /device:TPU:97, one launch (start us, length us, event | category | flops | bytes accessed | tf_op | source)
XLA Modules:
  0.0 1988.9 jit_solution(3852257070031251452)
XLA Ops:
  10.1 2.7 fusion.35
  13.8 2.7 copy-done.1
  16.5 2.4 fusion.27
  18.9 6.4 scatter-add.89
  26.7 4.4 add_select_fusion.1
  31.1 6.5 scatter-add.90
  39.0 2.4 fusion.24
  41.4 5.1 scatter-add.94
  46.5 2.4 fusion.23
  48.9 5.1 scatter-add.95
  55.5 2.4 fusion.20
  57.8 5.1 scatter-add.99
  63.0 2.4 fusion.19
  65.3 5.1 scatter-add.100
  70.6 2.9 collective-permute-start.8
  74.7 2.7 collective-permute-done.9
  81.4 1.6 scatter-add.104
  84.6 6.8 collective-permute-start
  91.4 1.9 collective-permute-start.1
  95.5 5.1 collective-permute-start.10
  100.6 1.9 collective-permute-start.11
  102.5 156.5 %all-gather.9.cloned.1.call-done = bf16[1,4096,256]{2,1,0:T(8,128)(2,1)} async-done(((bf16[1,64,256]{2,1,0:T(8,128)(2,1)}), bf16[1,4096,256]{2,1,0:T(8,128)(2,1)}) %all-gather.9.cloned.1.call-update) | async-done | bytes 2097168 | tf_op jit(solution)/shard_map/all_gather | solution.py:34
  259.0 2.5 gather_fusion
  263.0 3.3 collective-permute-start.3
  276.3 282.2 %all-gather.13.cloned.1.call-done = bf16[1,4096,256]{2,1,0:T(8,128)(2,1)} async-done(((bf16[1,64,256]{2,1,0:T(8,128)(2,1)}), bf16[1,4096,256]{2,1,0:T(8,128)(2,1)}) %all-gather.13.cloned.1.call-update) | async-done | bytes 2097168 | tf_op jit(solution)/shard_map/all_gather | solution.py:41
  558.5 3.9 bitcast_convert_fusion.1
  562.4 2.8 gather_fusion.2
  566.4 4.7 fusion.8
  571.7 49.7 %collective-permute-start.5 = (bf16[1,64,256]{2,1,0:T(8,128)(2,1)S(1)}, bf16[1,64,256]{2,1,0:T(8,128)(2,1)S(1)}, u32[]{:S(2)}, u32[]{:S(2)}) collective-permute-start(bf16[1,64,256]{2,1,0:T(8,128)(2,1)S(1)} %get-tuple-element.343), channel_id=1, source_target_pairs={{1,0},{2,1},{3,2},{5,4},{6,5},{7,6},{9,8},{10,9},{11,10},{13,12},{... | collective-permute-start | bytes 98312 | tf_op jit(solution)/shard_map/ppermute | solution.py:20
  621.4 4.2 collective-permute-start.4
  625.7 6.7 copy.30
  632.3 236.7 %all-gather.11.cloned.1.call-done = bf16[1,4096,256]{2,1,0:T(8,128)(2,1)} async-done(((bf16[1,64,256]{2,1,0:T(8,128)(2,1)}), bf16[1,4096,256]{2,1,0:T(8,128)(2,1)}) %all-gather.11.cloned.1.call-update) | async-done | bytes 2097168 | tf_op jit(solution)/shard_map/all_gather | solution.py:34
  869.0 2.5 gather_fusion.1
  873.0 3.1 collective-permute-start.7
  876.1 5.1 fusion.55
  882.5 2.2 copy-done.4
  884.7 6.7 copy.31
  891.4 5.1 fusion.56
  898.4 3.5 copy-done.2
  901.9 2.4 fusion.18
  904.3 6.4 scatter-add.110
  910.7 4.4 add_select_fusion
  915.1 6.5 scatter-add.111
  923.0 2.4 fusion.15
  925.4 5.1 scatter-add.115
  930.5 2.4 fusion.14
  932.9 5.1 scatter-add.116
  939.5 2.4 fusion.11
  941.9 5.1 scatter-add.120
  947.0 2.4 fusion.10
  949.4 5.1 scatter-add.121
  958.7 1.7 scatter-add.124
  961.4 1.7 scatter-add.125
  964.6 553.4 %all-reduce.7.cloned.1.call-done = (f32[3,3,256,256]{3,2,1,0:T(8,128)}, f32[3,3,256,256]{3,2,1,0:T(8,128)}) async-done(((f32[3,3,256,256]{3,2,1,0:T(8,128)}, f32[3,3,256,256]{3,2,1,0:T(8,128)}), (f32[3,3,256,256]{3,2,1,0:T(8,128)}, f32[3,3,256,256]{3,2,1,0:T(8,128)})) %all-reduce.7.cloned.1.call-update) | async-done | bytes 4718608 | tf_op jit(solution)/shard_map/psum | solution.py:137
  1518.8 52.4 %collective-permute-start.14 = (bf16[1,64,256]{2,1,0:T(8,128)(2,1)S(1)}, bf16[1,64,256]{2,1,0:T(8,128)(2,1)S(1)}, u32[]{:S(2)}, u32[]{:S(2)}) collective-permute-start(bf16[1,64,256]{2,1,0:T(8,128)(2,1)S(1)} %copy-done.10), channel_id=1, source_target_pairs={{0,1},{1,2},{2,3},{4,5},{5,6},{6,7},{8,9},{9,10},{10,11},{12,13},{... | collective-permute-start | bytes 98312 | tf_op jit(solution)/shard_map/ppermute | solution.py:18
  1571.2 1.9 collective-permute-start.15
  1574.2 3.7 collective-permute-done.15
  1578.6 238.5 %all-gather.15.cloned.1.call-done = bf16[1,4096,256]{2,1,0:T(8,128)(2,1)} async-done(((bf16[1,64,256]{2,1,0:T(8,128)(2,1)}), bf16[1,4096,256]{2,1,0:T(8,128)(2,1)}) %all-gather.15.cloned.1.call-update) | async-done | bytes 2097168 | tf_op jit(solution)/shard_map/all_gather | solution.py:41
  1817.1 3.9 bitcast_convert_fusion
  1821.0 3.1 gather_fusion.3
  1825.7 2.3 add_convert_fusion
  1828.0 4.5 fusion.1
  1832.5 144.6 %all-reduce.9.cloned.1.call-done = (f32[3,3,256,256]{3,2,1,0:T(8,128)}, f32[3,3,256,256]{3,2,1,0:T(8,128)}) async-done(((f32[3,3,256,256]{3,2,1,0:T(8,128)}, f32[3,3,256,256]{3,2,1,0:T(8,128)}), (f32[3,3,256,256]{3,2,1,0:T(8,128)}, f32[3,3,256,256]{3,2,1,0:T(8,128)})) %all-reduce.9.cloned.1.call-update) | async-done | bytes 4718608 | tf_op jit(solution)/shard_map/psum | solution.py:137
  1977.0 5.0 broadcast_multiply_fusion
  (147 shorter events, 48.4 us)
Async XLA Ops:
  7.2 559.2 %copy-start = (bf16[3,3,256,256]{3,2,1,0:T(8,128)(2,1)S(1)}, bf16[3,3,256,256]{3,2,1,0:T(8,128)(2,1)}, u32[]{:S(2)}) copy-start(bf16[3,3,256,256]{3,2,1,0:T(8,128)(2,1)} %param.65) | copy-start | bytes 3538948
  7.2 251.8 %all-gather.9.cloned.1.call-start = ((), (), s32[]{:S(2)}) async-start(), calls=%async_computation | async-start | bytes 2129920 | tf_op jit(solution)/shard_map/all_gather | solution.py:34
  8.7 549.8 %all-gather.13.cloned.1.call-start = ((), (), s32[]{:S(2)}) async-start(), calls=%async_computation.2 | async-start | bytes 2129920 | tf_op jit(solution)/shard_map/all_gather | solution.py:41
  8.8 4.0 copy-start.22
  12.8 3.7 copy-start.1
  16.4 9.5 copy-start.25
  70.6 6.8 copy-start.11
  70.6 6.8 copy-start.12
  70.6 4.1 collective-permute-start.8
  73.5 188.1 %copy-start.3 = (bf16[16,64,256]{2,1,0:T(8,128)(2,1)S(1)}, bf16[16,64,256]{2,1,0:T(8,128)(2,1)}, u32[]{:S(2)}) copy-start(bf16[16,64,256]{2,1,0:T(8,128)(2,1)} %param.64) | copy-start | bytes 1572868
  73.5 3.8 collective-permute-start.9
  74.7 2.7 copy-start.15
  77.3 0.6 copy-start.16
  84.5 181.8 %copy-start.9 = (bf16[1,64,256]{2,1,0:T(8,128)(2,1)S(1)}, bf16[1,64,256]{2,1,0:T(8,128)(2,1)}, u32[]{:S(2)}) copy-start(bf16[1,64,256]{2,1,0:T(8,128)(2,1)} %get-tuple-element.326) | copy-start | bytes 98308
  84.5 784.5 %all-gather.11.cloned.1.call-start = ((), (), s32[]{:S(2)}) async-start(), calls=%async_computation.1 | async-start | bytes 2129920 | tf_op jit(solution)/shard_map/all_gather | solution.py:34
  84.6 177.1 %collective-permute-start = (bf16[1,64,256]{2,1,0:T(8,128)(2,1)}, bf16[1,64,256]{2,1,0:T(8,128)(2,1)S(1)}, u32[]{:S(2)}, u32[]{:S(2)}) collective-permute-start(bf16[1,64,256]{2,1,0:T(8,128)(2,1)} %get-tuple-element.344), channel_id=1, source_target_pairs={{0,1},{1,2},{2,3},{4,5},{5,6},{6,7},{8,9},{9,10},{10,11},{12,13},{... | collective-permute-start | bytes 98312 | tf_op jit(solution)/shard_map/ppermute | solution.py:18
  91.4 170.1 %collective-permute-start.1 = (bf16[1,64,256]{2,1,0:T(8,128)(2,1)}, bf16[1,64,256]{2,1,0:T(8,128)(2,1)S(1)}, u32[]{:S(2)}, u32[]{:S(2)}) collective-permute-start(bf16[1,64,256]{2,1,0:T(8,128)(2,1)} %get-tuple-element.345), channel_id=1, source_target_pairs={{1,0},{2,1},{3,2},{5,4},{6,5},{7,6},{9,8},{10,9},{11,10},{13,12},{... | collective-permute-start | bytes 98312 | tf_op jit(solution)/shard_map/ppermute | solution.py:20
  94.1 777.4 %copy-start.19 = (pred[64]{0:T(512)(128)(4,1)}, pred[64]{0:T(512)(128)(4,1)S(1)}, u32[]{:S(2)}) copy-start(pred[64]{0:T(512)(128)(4,1)S(1)} %get-tuple-element.322) | copy-start | bytes 196
  94.1 774.9 %copy-start.21 = (s32[1024]{0:T(1024)}, s32[1024]{0:T(1024)S(1)}, u32[]{:S(2)}) copy-start(s32[1024]{0:T(1024)S(1)} %pad_clamp_fusion) | copy-start | bytes 12292
  95.5 170.8 %collective-permute-start.10 = (bf16[1,64,256]{2,1,0:T(8,128)(2,1)}, bf16[1,64,256]{2,1,0:T(8,128)(2,1)S(1)}, u32[]{:S(2)}, u32[]{:S(2)}) collective-permute-start(bf16[1,64,256]{2,1,0:T(8,128)(2,1)} %get-tuple-element.326), channel_id=1, source_target_pairs={{0,1},{1,2},{2,3},{4,5},{5,6},{6,7},{8,9},{9,10},{10,11},{12,13},{... | collective-permute-start | bytes 98312 | tf_op jit(solution)/shard_map/ppermute | solution.py:18
  100.6 165.7 %collective-permute-start.11 = (bf16[1,64,256]{2,1,0:T(8,128)(2,1)S(1)}, bf16[1,64,256]{2,1,0:T(8,128)(2,1)S(1)}, u32[]{:S(2)}, u32[]{:S(2)}) collective-permute-start(bf16[1,64,256]{2,1,0:T(8,128)(2,1)S(1)} %get-tuple-element.327), channel_id=1, source_target_pairs={{1,0},{2,1},{3,2},{5,4},{6,5},{7,6},{9,8},{10,9},{11,10},{13,12},{... | collective-permute-start | bytes 98312 | tf_op jit(solution)/shard_map/ppermute | solution.py:20
  261.7 5.7 collective-permute-start.2
  263.0 4.4 collective-permute-start.3
  276.3 290.0 %copy-start.17 = (s32[16,64]{1,0:T(8,128)S(1)}, s32[16,64]{1,0:T(8,128)}, u32[]{:S(2)}) copy-start(s32[16,64]{1,0:T(8,128)} %param.69) | copy-start | bytes 12292
  276.3 290.0 %copy-start.23 = (s32[256]{0:T(256)S(1)}, s32[256]{0:T(256)}, u32[]{:S(2)}) copy-start(s32[256]{0:T(256)} %copy-done.22) | copy-start | bytes 3076
  276.3 290.0 %copy-start.26 = (f32[256]{0:T(256)S(1)}, f32[256]{0:T(256)}, u32[]{:S(2)}) copy-start(f32[256]{0:T(256)} %param.66) | copy-start | bytes 3076
  565.4 1.0 copy-start.8
  571.7 946.4 %all-reduce.7.cloned.1.call-start = ((), (), s32[]{:S(2)}) async-start(), calls=%async_computation.4 | async-start | bytes 9437184 | tf_op jit(solution)/shard_map/psum | solution.py:137
  571.7 299.8 %collective-permute-start.5 = (bf16[1,64,256]{2,1,0:T(8,128)(2,1)S(1)}, bf16[1,64,256]{2,1,0:T(8,128)(2,1)S(1)}, u32[]{:S(2)}, u32[]{:S(2)}) collective-permute-start(bf16[1,64,256]{2,1,0:T(8,128)(2,1)S(1)} %get-tuple-element.343), channel_id=1, source_target_pairs={{1,0},{2,1},{3,2},{5,4},{6,5},{7,6},{9,8},{10,9},{11,10},{13,12},{... | collective-permute-start | bytes 98312 | tf_op jit(solution)/shard_map/ppermute | solution.py:20
  621.4 250.2 %collective-permute-start.4 = (bf16[1,64,256]{2,1,0:T(8,128)(2,1)}, bf16[1,64,256]{2,1,0:T(8,128)(2,1)S(1)}, u32[]{:S(2)}, u32[]{:S(2)}) collective-permute-start(bf16[1,64,256]{2,1,0:T(8,128)(2,1)} %get-tuple-element.342), channel_id=1, source_target_pairs={{0,1},{1,2},{2,3},{4,5},{5,6},{6,7},{8,9},{9,10},{10,11},{12,13},{... | collective-permute-start | bytes 98312 | tf_op jit(solution)/shard_map/ppermute | solution.py:18
  871.7 9.5 collective-permute-start.6
  873.0 8.3 collective-permute-start.7
  882.5 2.2 copy-start.4
  896.5 920.6 %all-gather.15.cloned.1.call-start = ((), (), s32[]{:S(2)}) async-start(), calls=%async_computation.3 | async-start | bytes 2129920 | tf_op jit(solution)/shard_map/all_gather | solution.py:41
  898.2 3.7 copy-start.2
  954.6 2.7 collective-permute-start.12
  954.7 3.9 collective-permute-start.13
  964.6 1012.5 %all-reduce.9.cloned.1.call-start = ((), (), s32[]{:S(2)}) async-start(), calls=%async_computation.5 | async-start | bytes 9437184 | tf_op jit(solution)/shard_map/psum | solution.py:137
  1518.1 0.8 copy-start.10
  1518.1 55.1 %copy-start.5 = (f32[18,64,256]{2,1,0:T(8,128)S(1)}, f32[18,64,256]{2,1,0:T(8,128)}, u32[]{:S(2)}) copy-start(f32[18,64,256]{2,1,0:T(8,128)} %scatter-add.125) | copy-start | bytes 3538948
  1518.8 55.4 %collective-permute-start.14 = (bf16[1,64,256]{2,1,0:T(8,128)(2,1)S(1)}, bf16[1,64,256]{2,1,0:T(8,128)(2,1)S(1)}, u32[]{:S(2)}, u32[]{:S(2)}) collective-permute-start(bf16[1,64,256]{2,1,0:T(8,128)(2,1)S(1)} %copy-done.10), channel_id=1, source_target_pairs={{0,1},{1,2},{2,3},{4,5},{5,6},{6,7},{8,9},{9,10},{10,11},{12,13},{... | collective-permute-start | bytes 98312 | tf_op jit(solution)/shard_map/ppermute | solution.py:18
  1571.2 6.7 collective-permute-start.15
  1574.2 242.9 %copy-start.13 = (bf16[1,64,256]{2,1,0:T(8,128)(2,1)}, bf16[1,64,256]{2,1,0:T(8,128)(2,1)S(1)}, u32[]{:S(2)}) copy-start(bf16[1,64,256]{2,1,0:T(8,128)(2,1)S(1)} %collective-permute-done.14) | copy-start | bytes 98308
  1577.9 239.2 %copy-start.14 = (bf16[1,64,256]{2,1,0:T(8,128)(2,1)}, bf16[1,64,256]{2,1,0:T(8,128)(2,1)S(1)}, u32[]{:S(2)}) copy-start(bf16[1,64,256]{2,1,0:T(8,128)(2,1)S(1)} %collective-permute-done.15) | copy-start | bytes 98308
  1578.6 245.5 %copy-start.20 = (pred[64]{0:T(512)(128)(4,1)S(1)}, pred[64]{0:T(512)(128)(4,1)}, u32[]{:S(2)}) copy-start(pred[64]{0:T(512)(128)(4,1)} %copy-done.19) | copy-start | bytes 196
  1578.6 247.1 %copy-start.6 = (bf16[16,64,256]{2,1,0:T(8,128)(2,1)S(1)}, bf16[16,64,256]{2,1,0:T(8,128)(2,1)}, u32[]{:S(2)}) copy-start(bf16[16,64,256]{2,1,0:T(8,128)(2,1)} %param.71) | copy-start | bytes 1572868
  1578.6 247.1 %copy-start.18 = (s32[16,64]{1,0:T(8,128)S(1)}, s32[16,64]{1,0:T(8,128)}, u32[]{:S(2)}) copy-start(s32[16,64]{1,0:T(8,128)} %param.69) | copy-start | bytes 12292
  1578.6 247.1 %copy-start.24 = (s32[256]{0:T(256)S(1)}, s32[256]{0:T(256)}, u32[]{:S(2)}) copy-start(s32[256]{0:T(256)} %copy-done.22) | copy-start | bytes 3076
  1821.0 6.9 copy-start.7
  1824.1 3.9 copy-start.27
Sparse Core Ops, SparseCore 0:
  10.3 248.6 all-gather.8
  261.4 297.1 all-gather.12
  571.8 297.1 all-gather.10
  896.7 621.3 all-reduce.6
  1520.3 296.7 all-gather.14
  1819.7 157.3 all-reduce.8
